TPU v7x, 32 devices: a whole 2x2x4 slice. The times are simulated.
32 devices in a mesh: row: 4 (over y, x), col: 8 (over z, core).
Axes of the slice: x: 2, y: 2, z: 4, core: 2. Of those that a mesh axis runs over, the one named last changes fastest.
Arguments:
- activations: bfloat16 [256, 16384], P(None, 'row'), may hold values from -3 to 3
- cotangent: bfloat16 [256, 16384], P(None, 'row'), may hold values from -0.59765625 to 0.59765625
- forget: int32 [256], replicated, may hold values 0 or 1
- lengths: int32 [4, 4], P('row'), may hold values from 1 to 32, 64 in all within a row
- query_weight: bfloat16 [16384, 8192], P('row', 'col'), may hold values from -0.046875 to 0.046875
- key_weight: bfloat16 [16384, 512], P('row'), may hold values from -0.046875 to 0.046875
- value_weight: bfloat16 [16384, 512], P('row'), may hold values from -0.046875 to 0.046875
- output_projection_weight: bfloat16 [8192, 16384], P('col', 'row'), may hold values from -0.0625 to 0.0625
- query_down: bfloat16 [16384, 32], P('row'), may hold values from -0.046875 to 0.046875
- query_up: bfloat16 [32, 8192], P(None, 'col'), may hold values from -1 to 1
- output_down: bfloat16 [8192, 32], P('col'), may hold values from -0.0625 to 0.0625
- output_up: bfloat16 [32, 16384], P(None, 'row'), may hold values from -1 to 1
Outputs:
- query_down_gradient: float32 [16384, 32], P('row')
- query_up_gradient: float32 [32, 8192], P(None, 'col')
- output_down_gradient: float32 [8192, 32], P('col')
- output_up_gradient: float32 [32, 16384], P(None, 'row')
Inputs may be any that keep to these rules, and one draw needn't show every extreme that they name: In every row of lengths the 4 values sum to 64, and the largest is exactly 32.
All inputs are finite; a program needn't handle non-finite values.
Results may differ from a plain program's by a relative error of at most 0.025.
Values may be sent and summed in bfloat16 or wider, within the bound.
A program may use at most 128 MiB of HBM per device.

v0:
```python
import math
import jax
import jax.numpy as jnp
from jax import lax
from jax.sharding import PartitionSpec as P

HD = 128
HEADS = 64
KVH = 4
adapter_scale = 0.5
highest_precision = lax.Precision.HIGHEST


def row_contraction(left, right):
    return lax.dot_general(
        left, right, (((1,), (1,)), ((), ())), preferred_element_type=jnp.float32
    )


def token_contraction(left, right):
    return lax.dot_general(
        left, right, (((0,), (0,)), ((), ())), preferred_element_type=jnp.float32
    )


def local(
    activations,
    cotangent,
    forget,
    lengths,
    query_weight,
    key_weight,
    value_weight,
    output_projection_weight,
    query_down,
    query_up,
    output_down,
    output_up,
):
    row_index = lax.axis_index("row")
    col_index = lax.axis_index("col")
    tok_blk = activations.shape[0] // lax.axis_size("row")
    query_cols = query_weight.shape[1]
    heads_dev = query_cols // HD
    group_index = col_index * heads_dev // (HEADS // KVH)
    inverse = 1.0 / math.sqrt(HD)
    up_projection_broad = query_up.astype(jnp.float32)
    down_projection_broad = output_down.astype(jnp.float32)
    key_slice = lax.dynamic_slice_in_dim(key_weight, group_index * HD, HD, 1)
    value_slice = lax.dynamic_slice_in_dim(value_weight, group_index * HD, HD, 1)
    kv_cols = key_slice.shape[1]
    block_of_rows = activations
    reduced_result = jnp.dot(block_of_rows, query_down, preferred_element_type=jnp.float32)
    query_partial_term = jnp.dot(block_of_rows, query_weight, preferred_element_type=jnp.float32)
    query_partial_term = query_partial_term + adapter_scale * jnp.dot(
        reduced_result, up_projection_broad, precision=highest_precision
    )
    key_term = jnp.dot(block_of_rows, key_slice, preferred_element_type=jnp.float32)
    value_term = jnp.dot(block_of_rows, value_slice, preferred_element_type=jnp.float32)
    summed = lax.psum_scatter(
        jnp.concatenate([query_partial_term, key_term, value_term, reduced_result], axis=1).astype(
            jnp.bfloat16
        ),
        "row",
        scatter_dimension=0,
        tiled=True,
    ).astype(jnp.float32)
    query_heads = summed[:, :query_cols].astype(jnp.bfloat16).reshape(tok_blk, heads_dev, HD)
    key_part = summed[:, query_cols : query_cols + kv_cols].astype(jnp.bfloat16)
    value_part = summed[:, query_cols + kv_cols : query_cols + 2 * kv_cols].astype(jnp.bfloat16)
    input_lowrank_factor = summed[:, query_cols + 2 * kv_cols :]
    seg_ends = jnp.cumsum(lengths[0])
    position = jnp.arange(tok_blk, dtype=jnp.int32)
    segment = jnp.sum((position[:, None] >= seg_ends[None, :]).astype(jnp.int32), axis=1)
    allowed = (segment[:, None] == segment[None, :]) & (position[None, :] <= position[:, None])
    scores = (
        jnp.einsum("qhd,kd->hqk", query_heads, key_part, preferred_element_type=jnp.float32)
        * inverse
    )
    numerator = jnp.where(allowed[None], jnp.exp(scores), 0.0)
    softmax = numerator / jnp.sum(numerator, axis=2, keepdims=True)
    weights = softmax.astype(jnp.bfloat16)
    hidden_state = jnp.einsum(
        "hqk,kd->qhd", weights, value_part, preferred_element_type=jnp.float32
    )
    hidden_state = hidden_state.reshape(tok_blk, query_cols).astype(jnp.bfloat16)
    sign_flip = (1 - 2 * forget).astype(jnp.bfloat16)
    output_gradient = cotangent * sign_flip[:, None]
    block_of_rows = output_gradient
    reduced_result = row_contraction(block_of_rows, output_up)
    hidden_state_term = row_contraction(
        block_of_rows, output_projection_weight
    ) + adapter_scale * jnp.dot(
        reduced_result, down_projection_broad.T, precision=highest_precision
    )
    backward = lax.psum_scatter(
        jnp.concatenate([hidden_state_term, reduced_result], axis=1).astype(jnp.bfloat16),
        "row",
        scatter_dimension=0,
        tiled=True,
    ).astype(jnp.float32)
    hidden_grad = backward[:, :query_cols].astype(jnp.bfloat16).reshape(tok_blk, heads_dev, HD)
    gradient_lowrank_factor = backward[:, query_cols:]
    prob_grad = jnp.einsum(
        "qhd,kd->hqk", hidden_grad, value_part, preferred_element_type=jnp.float32
    )
    score_grad = softmax * (prob_grad - jnp.sum(prob_grad * softmax, axis=2, keepdims=True))
    query_gradient = (
        jnp.einsum(
            "hqk,kd->qhd", score_grad, key_part.astype(jnp.float32), precision=highest_precision
        )
        * inverse
    )
    query_gradient = query_gradient.reshape(tok_blk, query_cols)
    query_lowrank_factor = jnp.dot(
        query_gradient, up_projection_broad.T, precision=highest_precision
    )
    hidden_state_factor = jnp.dot(hidden_state, output_down, preferred_element_type=jnp.float32)
    up_projection_piece = adapter_scale * jnp.dot(
        input_lowrank_factor.T, query_gradient, precision=highest_precision
    )
    down_projection_piece = adapter_scale * jnp.dot(
        hidden_state.astype(jnp.float32).T, gradient_lowrank_factor, precision=highest_precision
    )
    query_up_gradient, output_down_gradient = (
        lax.psum(up_projection_piece.astype(jnp.bfloat16), "row").astype(jnp.float32),
        lax.psum(down_projection_piece.astype(jnp.bfloat16), "row").astype(jnp.float32),
    )
    zero_rows = jnp.zeros((activations.shape[0], query_lowrank_factor.shape[1]), jnp.float32)
    first_token = row_index * tok_blk
    query_padded = lax.dynamic_update_slice_in_dim(zero_rows, query_lowrank_factor, first_token, 0)
    hidden_padded = lax.dynamic_update_slice_in_dim(zero_rows, hidden_state_factor, first_token, 0)
    query_total, hidden_total = lax.psum((query_padded, hidden_padded), ("row", "col"))
    query_everywhere = query_total.astype(jnp.bfloat16)
    hidden_state_everywhere = hidden_total.astype(jnp.bfloat16)
    query_down_gradient = adapter_scale * token_contraction(activations, query_everywhere)
    output_up_gradient = adapter_scale * token_contraction(hidden_state_everywhere, output_gradient)
    return (query_down_gradient, query_up_gradient, output_down_gradient, output_up_gradient)


def solution(mesh):
    placed = (
        P(None, "row"),
        P(None, "row"),
        P(),
        P("row", None),
        P("row", "col"),
        P("row", None),
        P("row", None),
        P("col", "row"),
        P("row", None),
        P(None, "col"),
        P("col", None),
        P(None, "row"),
    )
    return jax.shard_map(
        local,
        mesh=mesh,
        in_specs=placed,
        out_specs=(P("row", None), P(None, "col"), P("col", None), P(None, "row")),
        check_vma=False,
    )
```

profile of v0, /device:TPU:0, one launch (start us, length us, event | category | flops | bytes accessed | tf_op | source)
XLA Modules:
  0.0 180.6 jit_solution(12886477900674417634)
XLA Ops:
  7.2 1.5 copy-done
  8.8 1.7 fusion.58
  10.5 0.1 copy.46
  10.6 1.9 %fusion.17 = bf16[256,128]{1,0:T(8,128)(2,1)S(1)} fusion(bf16[256,4096]{1,0:T(8,128)(2,1)S(1)} %copy-done, bf16[4096,512]{1,0:T(8,128)(2,1)} %param.17, s32[]{:T(128)S(6)} %select_n.18), kind=kOutput, calls=%fused_computation.29 | convolution fusion | flops 268468224 | bytes 3211268 | tf_op jit(solution)/shard_map/dot_general | solution.py:58
  12.5 1.9 %fusion.18 = bf16[256,128]{1,0:T(8,128)(2,1)S(1)} fusion(bf16[256,4096]{1,0:T(8,128)(2,1)S(1)} %copy-done, bf16[4096,512]{1,0:T(8,128)(2,1)} %param.18, s32[]{:T(128)S(6)} %select_n.18), kind=kOutput, calls=%fused_computation.30 | convolution fusion | flops 268468224 | bytes 3211268 | tf_op jit(solution)/shard_map/dot_general | solution.py:59
  14.4 5.7 %fusion.60 = f32[256,1024]{1,0:T(8,128)S(1)} fusion(bf16[256,4096]{1,0:T(8,128)(2,1)S(1)} %copy-done, bf16[4096,1024]{1,0:T(8,128)(2,1)} %param.16), kind=kOutput, calls=%fused_computation.79 | convolution fusion | flops 2147483648 | bytes 11534336 | tf_op jit(solution)/shard_map/dot_general | solution.py:54
  20.2 0.7 fusion.8
  20.9 0.9 pad_maximum_fusion
  21.9 2.4 %fusion.59 = (bf16[256,32]{0,1:T(8,128)(2,1)S(1)}, f32[256,32]{0,1:T(8,128)S(1)}) fusion(bf16[32,4096]{1,0:T(8,128)(2,1)S(1)} %copy-done.3, bf16[256,4096]{1,0:T(8,128)(2,1)} %param.13, bf16[256]{0:T(256)(128)(2,1)S(1)} %subtract_convert_fusion), kind=kOutput, calls=%fused_computation.78 | convolution fusion | flops 68165632 | bytes 2408960 | tf_op jit(solution)/shard_map/dot_general | solution.py:15
  24.3 0.1 copy.48
  24.5 6.4 %fusion.4 = f32[256,1024]{1,0:T(8,128)S(1)} fusion(bf16[1024,4096]{1,0:T(8,128)(2,1)} %param.19, bf16[256,4096]{1,0:T(8,128)(2,1)} %param.13, bf16[256]{0:T(256)(128)(2,1)S(1)} %subtract_convert_fusion), kind=kOutput, calls=%fused_computation.6 | convolution fusion | flops 2148532224 | bytes 11534848 | tf_op jit(solution)/shard_map/dot_general | solution.py:15
  30.9 0.6 fusion.9
  31.5 0.9 pad_maximum_fusion.1
  32.5 0.2 reduce-window.8
  32.8 17.6 %reduce-scatter.3.cloned.1.call-done = bf16[64,1312]{1,0:T(8,128)(2,1)} async-done(((bf16[256,1312]{1,0:T(8,128)(2,1)}), bf16[64,1312]{1,0:T(8,128)(2,1)}) %reduce-scatter.3.cloned.1.call-update) | async-done | bytes 167952 | tf_op jit(solution)/shard_map/reduce_scatter | solution.py:60
  50.4 1.2 fusion.41
  51.7 0.9 fusion.14
  52.6 0.1 fusion.31
  52.7 25.9 %reduce-scatter.5.cloned.1.call-done = bf16[64,1056]{1,0:T(8,128)(2,1)} async-done(((bf16[256,1056]{1,0:T(8,128)(2,1)}), bf16[64,1056]{1,0:T(8,128)(2,1)}) %reduce-scatter.5.cloned.1.call-update) | async-done | bytes 135184 | tf_op jit(solution)/shard_map/reduce_scatter | solution.py:96
  78.7 1.2 multiply_reduce_fusion
  79.8 1.1 fusion.10
  81.0 0.3 fusion.25
  81.2 0.3 dynamic_update_slice.7
  81.6 0.3 dynamic_update_slice.6
  82.0 39.9 %all-reduce = (bf16[256,32]{0,1:T(8,128)(2,1)S(1)}, bf16[256,32]{0,1:T(8,128)(2,1)S(1)}) all-reduce(f32[256,32]{0,1:T(8,128)S(1)} %dynamic_update_slice.6, f32[256,32]{0,1:T(8,128)S(1)} %dynamic_update_slice.7), channel_id=1, replica_groups=mesh['row'=4,'col'=8] {'row','col'}, use_global_device_ids=true, to_apply=%region_6.7 | all-reduce | flops 16384 | bytes 98304 | tf_op jit(solution)/shard_map/psum | solution.py:133
  121.9 2.9 %convolution_multiply_fusion = f32[32,4096]{1,0:T(8,128)} fusion(bf16[256,4096]{1,0:T(8,128)(2,1)} %param.13, bf16[256]{0:T(256)(128)(2,1)S(1)} %subtract_convert_fusion, bf16[256,32]{0,1:T(8,128)(2,1)S(1)} %get-tuple-element.5), kind=kOutput, calls=%fused_computation | convolution fusion | flops 68288512 | bytes 2638336 | tf_op jit(solution)/shard_map/dot_general | solution.py:21
  124.8 1.6 fusion.16
  126.4 1.6 fusion.15
  128.0 1.3 fusion
  129.2 41.8 %all-reduce.4.cloned.1.call-done = (bf16[32,1024]{1,0:T(8,128)(2,1)}, bf16[1024,32]{0,1:T(8,128)(2,1)}) async-done(((bf16[32,1024]{1,0:T(8,128)(2,1)}, bf16[1024,32]{0,1:T(8,128)(2,1)}), (bf16[32,1024]{1,0:T(8,128)(2,1)}, bf16[1024,32]{0,1:T(8,128)(2,1)})) %all-reduce.4.cloned.1.call-update) | async-done | bytes 131088 | tf_op jit(solution)/shard_map/psum | solution.py:126
  171.0 1.5 convert_element_type.52
  172.5 1.5 convert_element_type.58
  (22 shorter events, 0.4 us)
Async XLA Ops:
  7.2 1.6 copy-start
  7.2 43.3 %reduce-scatter.3.cloned.1.call-start = ((), (), s32[]{:S(2)}) async-start(), calls=%async_computation.2 | async-start | bytes 901120 | tf_op jit(solution)/shard_map/reduce_scatter | solution.py:60
  14.4 5.8 %copy-start.1 = (bf16[32,1024]{1,0:T(8,128)(2,1)S(1)}, bf16[32,1024]{1,0:T(8,128)(2,1)}, u32[]{:S(2)}) copy-start(bf16[32,1024]{1,0:T(8,128)(2,1)} %param.21) | copy-start | bytes 196612
  20.2 1.7 copy-start.4
  20.2 1.7 copy-start.3
  21.8 56.8 %reduce-scatter.5.cloned.1.call-start = ((), (), s32[]{:S(2)}) async-start(), calls=%async_computation.3 | async-start | bytes 737280 | tf_op jit(solution)/shard_map/reduce_scatter | solution.py:96
  24.5 6.4 %copy-start.2 = (bf16[1024,32]{0,1:T(8,128)(2,1)S(1)}, bf16[1024,32]{0,1:T(8,128)(2,1)}, u32[]{:S(2)}) copy-start(bf16[1024,32]{0,1:T(8,128)(2,1)} %param.22) | copy-start | bytes 196612
  30.9 1.6 copy-start.5
  32.4 138.6 %all-reduce.4.cloned.1.call-start = ((), (), s32[]{:S(2)}) async-start(), calls=%async_computation.4 | async-start | bytes 262144 | tf_op jit(solution)/shard_map/psum | solution.py:126
Sparse Core Ops, SparseCore 0:
  22.0 28.4 reduce-scatter.2
  53.6 25.0 reduce-scatter.4
  128.1 42.8 all-reduce.3
where the time goes:
time: 181 us
  waiting for transfers between devices  85.3 us (47%)
  blocking collectives  39.9 us (22%)
  matrix products  33.5 us (19%)
  between operations  14 us (8%)
  other arithmetic  5.14 us (3%)
  local copies, waits for them, and re-layouts  2.51 us (1%)
    psum x1, waiting for transfers between devices, local(): lax.psum(up_projection_piece.astype(jnp.bfloat16), 'row')  41.8 us
    psum x1, blocking collectives, local(): lax.psum((query_padded, hidden_padded), ('row', 'col'))  39.9 us
    reduce_scatter x1, waiting for transfers between devices, local(): lax.psum_scatter(jnp.concatenate([hidden_state_term, reduced_result], axi...  25.9 us
    reduce_scatter x1, waiting for transfers between devices, local(): lax.psum_scatter(jnp.concatenate([query_partial_term, key_term, value_ter...  17.6 us
    dot_general x2, matrix products, row_contraction(): lax.dot_general(left, right, (((1,), (1,)), ((), ())), preferred_element_...  8.79 us
    dot_general x1, matrix products, local(): jnp.dot(block_of_rows, query_weight, preferred_element_type=jnp.float32)  5.74 us
    dot_general x2, matrix products, token_contraction(): lax.dot_general(left, right, (((0,), (0,)), ((), ())), preferred_element_...  4.2 us
  transfers between devices with their start and end apart: 3, of which 3 were waited for; matrix products, arithmetic and copies ran while one was open for 8% of the time, Pallas kernels for 0%

commit v1 on v0

--- a/solution.py
+++ b/solution.py
@@ -123,7 +123,9 @@
         hidden_state.astype(jnp.float32).T, gradient_lowrank_factor, precision=highest_precision
     )
     query_up_gradient, output_down_gradient = (
-        lax.psum(up_projection_piece.astype(jnp.bfloat16), "row").astype(jnp.float32),
+        jnp.sum(lax.all_gather(up_projection_piece.astype(jnp.bfloat16), "row"), axis=0).astype(
+            jnp.float32
+        ),
         lax.psum(down_projection_piece.astype(jnp.bfloat16), "row").astype(jnp.float32),
     )
     zero_rows = jnp.zeros((activations.shape[0], query_lowrank_factor.shape[1]), jnp.float32)

time: 181 us -> 147 us (0.81)
  waiting for transfers between devices: 85.3 us -> 43.6 us
  blocking collectives: 39.9 us -> 49.9 us
  matrix products: 33.5 us -> 31.3 us
    psum x1, waiting for transfers between devices: 41.8 us -> 0.01 us  [local(): lax.psum(down_projection_piece.astype(jnp.bfloat16), 'row')]
    all_gather x0 -> x1, blocking collectives: none -> 10 us  [local(): lax.all_gather(up_projection_piece.astype(jnp.bfloat16), 'row')]
  transfers between devices with their start and end apart: 3 -> 3, of which waited for: 3 -> 2; matrix products, arithmetic and copies ran while one was open for 8% -> 14% of each run, Pallas kernels for 0% -> 0%
where the time goes in v1:
time: 147 us; the launch traced here: 146 us
  blocking collectives  49.9 us (34%)
  waiting for transfers between devices  43.6 us (30%)
  matrix products  31.3 us (21%)
  between operations  14 us (10%)
  other arithmetic  4.35 us (3%)
  local copies, waits for them, and re-layouts  3.02 us (2%)
    psum x1, blocking collectives, local(): lax.psum((query_padded, hidden_padded), ('row', 'col'))  39.9 us
    reduce_scatter x1, waiting for transfers between devices, local(): lax.psum_scatter(jnp.concatenate([hidden_state_term, reduced_result], axi...  25.9 us
    reduce_scatter x1, waiting for transfers between devices, local(): lax.psum_scatter(jnp.concatenate([query_partial_term, key_term, value_ter...  17.6 us
    all_gather x1, blocking collectives, local(): lax.all_gather(up_projection_piece.astype(jnp.bfloat16), 'row')  10 us
    dot_general x2, matrix products, row_contraction(): lax.dot_general(left, right, (((1,), (1,)), ((), ())), preferred_element_...  8.79 us
    dot_general x1, matrix products, local(): jnp.dot(block_of_rows, query_weight, preferred_element_type=jnp.float32)  5.74 us
  transfers between devices with their start and end apart: 3, of which 2 were waited for; matrix products, arithmetic and copies ran while one was open for 14% of the time, Pallas kernels for 0%

profile of v1, /device:TPU:0, one launch (start us, length us, event | category | flops | bytes accessed | tf_op | source)
XLA Modules:
  0.0 146.3 jit_solution(2194071299659625554)
XLA Ops:
  7.2 1.5 %copy-done = bf16[256,4096]{1,0:T(8,128)(2,1)S(1)} copy-done((bf16[256,4096]{1,0:T(8,128)(2,1)S(1)}, bf16[256,4096]{1,0:T(8,128)(2,1)}, u32[]{:S(2)}) %copy-start) | copy-done | bytes 2097176
  8.8 1.7 %fusion.58 = (bf16[256,32]{0,1:T(8,128)(2,1)S(1)}, f32[256,32]{0,1:T(8,128)S(1)}) fusion(bf16[256,4096]{1,0:T(8,128)(2,1)S(1)} %copy-done, bf16[4096,32]{0,1:T(8,128)(2,1)} %param.20), kind=kOutput, calls=%fused_computation.77 | convolution fusion | flops 67117056 | bytes 2408448 | tf_op jit(solution)/shard_map/dot_general | solution.py:53
  10.6 1.9 %fusion.17 = bf16[256,128]{1,0:T(8,128)(2,1)S(1)} fusion(bf16[256,4096]{1,0:T(8,128)(2,1)S(1)} %copy-done, bf16[4096,512]{1,0:T(8,128)(2,1)} %param.17, s32[]{:T(128)S(6)} %select_n.18), kind=kOutput, calls=%fused_computation.29 | convolution fusion | flops 268468224 | bytes 3211268 | tf_op jit(solution)/shard_map/dot_general | solution.py:58
  12.5 1.9 %fusion.18 = bf16[256,128]{1,0:T(8,128)(2,1)S(1)} fusion(bf16[256,4096]{1,0:T(8,128)(2,1)S(1)} %copy-done, bf16[4096,512]{1,0:T(8,128)(2,1)} %param.18, s32[]{:T(128)S(6)} %select_n.18), kind=kOutput, calls=%fused_computation.30 | convolution fusion | flops 268468224 | bytes 3211268 | tf_op jit(solution)/shard_map/dot_general | solution.py:59
  14.4 5.7 %fusion.60 = f32[256,1024]{1,0:T(8,128)S(1)} fusion(bf16[256,4096]{1,0:T(8,128)(2,1)S(1)} %copy-done, bf16[4096,1024]{1,0:T(8,128)(2,1)} %param.16), kind=kOutput, calls=%fused_computation.79 | convolution fusion | flops 2147483648 | bytes 11534336 | tf_op jit(solution)/shard_map/dot_general | solution.py:54
  20.2 0.7 fusion.8
  20.9 0.9 pad_maximum_fusion
  21.9 2.4 %fusion.59 = (bf16[256,32]{0,1:T(8,128)(2,1)S(1)}, f32[256,32]{0,1:T(8,128)S(1)}) fusion(bf16[32,4096]{1,0:T(8,128)(2,1)S(1)} %copy-done.4, bf16[256,4096]{1,0:T(8,128)(2,1)} %param.13, bf16[256]{0:T(256)(128)(2,1)S(1)} %subtract_convert_fusion), kind=kOutput, calls=%fused_computation.78 | convolution fusion | flops 68165632 | bytes 2408960 | tf_op jit(solution)/shard_map/dot_general | solution.py:15
  24.3 0.1 copy.48
  24.5 6.4 %fusion.4 = f32[256,1024]{1,0:T(8,128)S(1)} fusion(bf16[1024,4096]{1,0:T(8,128)(2,1)} %param.19, bf16[256,4096]{1,0:T(8,128)(2,1)} %param.13, bf16[256]{0:T(256)(128)(2,1)S(1)} %subtract_convert_fusion), kind=kOutput, calls=%fused_computation.6 | convolution fusion | flops 2148532224 | bytes 11534848 | tf_op jit(solution)/shard_map/dot_general | solution.py:15
  30.9 0.6 fusion.9
  31.5 0.9 pad_maximum_fusion.1
  32.5 0.2 reduce-window.8
  32.8 17.6 %reduce-scatter.3.cloned.1.call-done = bf16[64,1312]{1,0:T(8,128)(2,1)} async-done(((bf16[256,1312]{1,0:T(8,128)(2,1)}), bf16[64,1312]{1,0:T(8,128)(2,1)}) %reduce-scatter.3.cloned.1.call-update) | async-done | bytes 167952 | tf_op jit(solution)/shard_map/reduce_scatter | solution.py:60
  50.4 1.2 fusion.41
  51.7 0.9 fusion.14
  52.6 0.1 fusion.31
  52.7 25.9 %reduce-scatter.5.cloned.1.call-done = bf16[64,1056]{1,0:T(8,128)(2,1)} async-done(((bf16[256,1056]{1,0:T(8,128)(2,1)}), bf16[64,1056]{1,0:T(8,128)(2,1)}) %reduce-scatter.5.cloned.1.call-update) | async-done | bytes 135184 | tf_op jit(solution)/shard_map/reduce_scatter | solution.py:96
  78.7 1.6 %fusion.16 = bf16[1024,32]{0,1:T(8,128)(2,1)} fusion(bf16[8,8,8,128]{3,2,1,0:T(8,128)(2,1)S(1)} %fusion.14, bf16[64,1056]{1,0:T(8,128)(2,1)} %reduce-scatter.5.cloned.1.call-done), kind=kOutput, calls=%fused_computation.28 | convolution fusion | flops 4259840 | bytes 212992 | tf_op jit(solution)/shard_map/dot_general | solution.py:122
  80.2 1.2 multiply_reduce_fusion
  81.4 1.1 fusion.10
  82.5 0.3 fusion.25
  82.8 0.3 dynamic_update_slice.7
  83.2 0.3 dynamic_update_slice.6
  83.5 39.9 %all-reduce = (bf16[256,32]{0,1:T(8,128)(2,1)S(1)}, bf16[256,32]{0,1:T(8,128)(2,1)S(1)}) all-reduce(f32[256,32]{0,1:T(8,128)S(1)} %dynamic_update_slice.6, f32[256,32]{0,1:T(8,128)S(1)} %dynamic_update_slice.7), channel_id=1, replica_groups=mesh['row'=4,'col'=8] {'row','col'}, use_global_device_ids=true, to_apply=%region_6.7 | all-reduce | flops 16384 | bytes 98304 | tf_op jit(solution)/shard_map/psum | solution.py:135
  123.5 1.3 fusion
  124.7 0.5 copy-done.1
  125.2 1.3 convolution_multiply_fusion
  126.6 1.0 fusion.15
  127.5 10.0 %all-gather = bf16[128,1024]{1,0:T(8,128)(2,1)S(1)} all-gather(bf16[32,1024]{1,0:T(8,128)(2,1)S(1)} %fusion.15), channel_id=2, replica_groups=mesh['row'=4,'col'=8] {'row'}, dimensions={0}, use_global_device_ids=true | all-gather | bytes 327680 | tf_op jit(solution)/shard_map/all_gather | solution.py:126
  137.6 0.7 convert_element_type.54
  138.3 1.5 %convert_element_type.60 = f32[1024,32]{0,1:T(8,128)} convert(bf16[1024,32]{0,1:T(8,128)(2,1)} %all-reduce.3.cloned.1.call-done) | non-fusion elementwise | flops 32768 | bytes 196608 | tf_op jit(solution)/shard_map/convert_element_type | solution.py:129
  (26 shorter events, 0.6 us)
Async XLA Ops:
  7.2 1.6 %copy-start = (bf16[256,4096]{1,0:T(8,128)(2,1)S(1)}, bf16[256,4096]{1,0:T(8,128)(2,1)}, u32[]{:S(2)}) copy-start(bf16[256,4096]{1,0:T(8,128)(2,1)} %param.12) | copy-start | bytes 6291460
  7.2 43.3 %reduce-scatter.3.cloned.1.call-start = ((), (), s32[]{:S(2)}) async-start(), calls=%async_computation.2 | async-start | bytes 901120 | tf_op jit(solution)/shard_map/reduce_scatter | solution.py:60
  14.4 5.8 %copy-start.2 = (bf16[32,1024]{1,0:T(8,128)(2,1)S(1)}, bf16[32,1024]{1,0:T(8,128)(2,1)}, u32[]{:S(2)}) copy-start(bf16[32,1024]{1,0:T(8,128)(2,1)} %param.21) | copy-start | bytes 196612
  20.2 1.7 %copy-start.5 = (s32[256]{0:T(256)S(1)}, s32[256]{0:T(256)}, u32[]{:S(2)}) copy-start(s32[256]{0:T(256)} %param.14) | copy-start | bytes 3076
  20.2 1.7 %copy-start.4 = (bf16[32,4096]{1,0:T(8,128)(2,1)S(1)}, bf16[32,4096]{1,0:T(8,128)(2,1)}, u32[]{:S(2)}) copy-start(bf16[32,4096]{1,0:T(8,128)(2,1)} %param.23) | copy-start | bytes 786436
  21.8 56.8 %reduce-scatter.5.cloned.1.call-start = ((), (), s32[]{:S(2)}) async-start(), calls=%async_computation.3 | async-start | bytes 737280 | tf_op jit(solution)/shard_map/reduce_scatter | solution.py:96
  24.5 6.4 %copy-start.3 = (bf16[1024,32]{0,1:T(8,128)(2,1)S(1)}, bf16[1024,32]{0,1:T(8,128)(2,1)}, u32[]{:S(2)}) copy-start(bf16[1024,32]{0,1:T(8,128)(2,1)} %param.22) | copy-start | bytes 196612
  30.9 1.6 %copy-start.6 = (s32[1,4]{1,0:T(1,128)S(1)}, s32[1,4]{1,0:T(1,128)}, u32[]{:S(2)}) copy-start(s32[1,4]{1,0:T(1,128)} %param.15) | copy-start | bytes 52
  32.4 105.8 %all-reduce.3.cloned.1.call-start = ((), (), s32[]{:S(2)}) async-start(), calls=%async_computation.4 | async-start | bytes 131072 | tf_op jit(solution)/shard_map/psum | solution.py:129
  123.4 1.8 %copy-start.1 = (bf16[256,4096]{1,0:T(8,128)(2,1)S(1)}, bf16[256,4096]{1,0:T(8,128)(2,1)}, u32[]{:S(2)}) copy-start(bf16[256,4096]{1,0:T(8,128)(2,1)} %param.13) | copy-start | bytes 6291460
Sparse Core Ops, SparseCore 0:
  22.0 28.4 reduce-scatter.2
  53.6 25.0 reduce-scatter.4
  82.1 41.4 all-reduce.2
